TPU v7x, 32 devices: a whole 2x2x4 slice. The times are simulated.
32 devices in a mesh: league: 4 (over x, core), env: 8 (over z, y).
Axes of the slice: x: 2, y: 2, z: 4, core: 2. Of those that a mesh axis runs over, the one named last changes fastest.
Arguments:
- obs_own: bfloat16 [4, 2, 128, 16, 2048], P('league', None, 'env'), may hold values from -6 to 6
- obs_opp: bfloat16 [4, 2, 128, 16, 2048], P('league', None, 'env'), may hold values from -6 to 6
- actions: int32 [4, 2, 2, 128, 16], P('league', None, None, 'env'), may hold values from 0 to 255
- opponent_picks: int32 [4, 2], P('league'), may hold values from 0 to 3
- policy_weight: bfloat16 [4, 2048, 2048], P('league', 'env'), may hold values from -0.125 to 0.125
- policy_gain: bfloat16 [4, 2048], P('league'), may hold values from 0.25 to 1.75
- action_table: bfloat16 [256, 2048], replicated, may hold values from -6 to 6
- value_gain: bfloat16 [2048], replicated, may hold values from 0.25 to 1.75
- value_up: bfloat16 [2048, 1024], replicated, may hold values from -0.125 to 0.125
- value_out: bfloat16 [1024], replicated, may hold values from -0.1875 to 0.1875
Outputs:
- learner_rows: bfloat16 [4, 2, 16, 2048, 128], P('league', None, None, 'env')
- values: float32 [4, 2, 128, 16], P('league', None, 'env')
All inputs are finite; a program needn't handle non-finite values.
Results may differ from a plain program's by a relative error of at most 0.0054.
Values may be sent and summed in bfloat16 or wider, within the bound.
A program may use at most 128 MiB of HBM per device.

v0:
```python
import jax
import jax.numpy as jnp
from jax import lax
from jax.sharding import PartitionSpec as P


def rms_norm(inputs, gain):
    scale = lax.rsqrt(jnp.mean(inputs * inputs, axis=-1, keepdims=True) + 1e-05)
    return inputs * scale * gain.astype(jnp.float32)


def local(
    obs_own,
    obs_opp,
    actions,
    opponent_picks,
    policy_weight,
    policy_gain,
    action_table,
    value_gain,
    value_up,
    value_out,
):
    round_count = obs_own.shape[1]
    env_count = obs_own.shape[2]
    step_count = obs_own.shape[3]
    model_width = obs_own.shape[4]
    row_count = env_count * step_count
    weight_shard = policy_weight[0]
    own_gain = policy_gain[0]
    group_count = lax.axis_size("league")
    my_group = lax.axis_index("league")
    own_inputs = obs_own[0].reshape(round_count * row_count, model_width).astype(jnp.float32)
    own_normed = rms_norm(own_inputs, own_gain).astype(jnp.bfloat16)
    own_whole = lax.all_gather(weight_shard, "env", axis=0, tiled=True)
    own_state = own_inputs + jnp.dot(own_normed, own_whole, preferred_element_type=jnp.float32)
    every_pick = lax.all_gather(opponent_picks, "league", axis=0, tiled=True)
    action_range = jnp.arange(action_table.shape[0], dtype=jnp.int32)
    traj_list = []
    value_list = []
    for round_index in range(round_count):
        opp_raw = obs_opp[0, round_index].reshape(row_count, model_width)
        opp_inputs = opp_raw.astype(jnp.float32)
        all_rows = lax.all_gather(opp_raw, "league", axis=0, tiled=True)
        all_normed = rms_norm(all_rows.astype(jnp.float32), own_gain).astype(jnp.bfloat16)
        products = jnp.dot(all_normed, own_whole, preferred_element_type=jnp.float32)
        served = (every_pick[:, round_index] == my_group).astype(jnp.float32)
        products = (
            products.reshape(group_count, row_count, model_width) * served[:, None, None]
        ).reshape(group_count * row_count, model_width)
        opp_state = opp_inputs + lax.psum_scatter(
            products, "league", scatter_dimension=0, tiled=True
        )
        own_ids = actions[0, 0, round_index].reshape(row_count)
        opp_ids = actions[0, 1, round_index].reshape(row_count)
        onehot = (own_ids[:, None] == action_range[None, :]).astype(jnp.bfloat16) + (
            opp_ids[:, None] == action_range[None, :]
        ).astype(jnp.bfloat16)
        action_sum = jnp.dot(onehot, action_table, preferred_element_type=jnp.float32)
        round_state = lax.dynamic_slice_in_dim(own_state, round_index * row_count, row_count, 0)
        joint_sum = round_state + opp_state + action_sum
        joint_row = rms_norm(joint_sum, value_gain).astype(jnp.bfloat16)
        value_hidden = jax.nn.silu(
            jnp.dot(joint_row, value_up, preferred_element_type=jnp.float32)
        ).astype(jnp.bfloat16)
        value_est = jnp.dot(value_hidden, value_out, preferred_element_type=jnp.float32)
        value_list.append(value_est.reshape(env_count, step_count))
        time_block = joint_row.reshape(env_count, step_count, model_width).transpose(1, 2, 0)
        traj_list.append(lax.all_to_all(time_block, "env", split_axis=1, concat_axis=2, tiled=True))
    learner_rows = jnp.stack(traj_list)
    values = jnp.stack(value_list)
    return (learner_rows[None], values[None])


def solution(mesh):
    in_specs = (
        P("league", None, "env", None, None),
        P("league", None, "env", None, None),
        P("league", None, None, "env", None),
        P("league", None),
        P("league", "env", None),
        P("league", None),
        P(),
        P(),
        P(),
        P(),
    )
    out_specs = (P("league", None, None, "env", None), P("league", None, "env", None))
    return jax.shard_map(local, mesh=mesh, in_specs=in_specs, out_specs=out_specs, check_vma=False)
```

profile of v0, /device:TPU:0, one launch (start us, length us, event | category | flops | bytes accessed | tf_op | source)
XLA Modules:
  0.0 480.6 jit_solution(18280044370628031255)
XLA Ops:
  7.2 0.0 copy-start
  7.2 0.0 all-gather.6.cloned.1.call-start
  7.2 3.2 fusion.49
  10.4 0.0 all-gather.6.cloned.1.call-update
  10.5 0.0 all-gather.10.cloned.1.call-start
  10.5 0.7 all-gather.10.cloned.1.call-update
  11.2 0.0 all-gather.8.cloned.1.call-start
  11.3 0.7 all-gather.8.cloned.1.call-update
  12.0 0.0 reduce-scatter.3.cloned.1.call-start
  12.0 6.0 %all-gather.1 = s32[4,1,2]{2,1,0:T(1,128)S(1)} all-gather(s32[1,1,2]{2,1,0:T(1,128)S(1)} %bitcast.98), channel_id=1, replica_groups=mesh['league'=4,'env'=8] {'league'}, dimensions={0}, use_global_device_ids=true | all-gather | bytes 40 | tf_op jit(solution)/shard_map/all_gather | solution.py:37
  18.0 0.1 copy.23
  18.1 0.1 broadcast_bitcast_fusion
  18.2 0.0 copy-done.10
  18.2 29.6 %all-gather.6.cloned.1.call-done = bf16[1024,2048]{1,0:T(8,128)(2,1)} async-done(((bf16[256,2048]{1,0:T(8,128)(2,1)}), bf16[1024,2048]{1,0:T(8,128)(2,1)}) %all-gather.6.cloned.1.call-update) | async-done | bytes 4194320 | tf_op jit(solution)/shard_map/all_gather | solution.py:44
  47.8 3.1 fusion
  50.9 124.0 %all-gather.10.cloned.1.call-done = bf16[1,2048,2048]{2,1,0:T(8,128)(2,1)} async-done(((bf16[1,256,2048]{2,1,0:T(8,128)(2,1)}), bf16[1,2048,2048]{2,1,0:T(8,128)(2,1)}) %all-gather.10.cloned.1.call-update) | async-done | bytes 8388624 | tf_op jit(solution)/shard_map/all_gather | solution.py:35
  174.9 14.5 %fusion.12 = f32[1024,2048]{1,0:T(8,128)} fusion(bf16[1,2048,2048]{2,1,0:T(8,128)(2,1)} %all-gather.10.cloned.1.call-done, bf16[1024,2048]{1,0:T(8,128)(2,1)} %all-gather.6.cloned.1.call-done, f32[1024]{0:T(1024)S(1)} %bitcast.94, f32[2048]{0:T(1024)S(1)} %bitcast.90, f32[1024]{0:T(1024)S(1)} %add_rsqrt_fusion.2), kind=kOutput, calls=%fused_computation.16 | convolution fusion | flops 8600420352 | bytes 20987904 | tf_op jit(solution)/shard_map/dot_general | solution.py:46
  189.4 0.0 reduce-scatter.3.cloned.1.call-update
  189.5 0.2 reduce-scatter.5.cloned.1.call-start
  189.7 19.5 %all-gather.8.cloned.1.call-done = bf16[1024,2048]{1,0:T(8,128)(2,1)} async-done(((bf16[256,2048]{1,0:T(8,128)(2,1)}), bf16[1024,2048]{1,0:T(8,128)(2,1)}) %all-gather.8.cloned.1.call-update) | async-done | bytes 4194320 | tf_op jit(solution)/shard_map/all_gather | solution.py:44
  209.2 3.2 fusion.3
  212.4 0.2 copy-done.6
  212.6 13.6 %fusion.15 = f32[1024,2048]{1,0:T(8,128)} fusion(bf16[1,2048,2048]{2,1,0:T(8,128)(2,1)} %all-gather.10.cloned.1.call-done, bf16[1024,2048]{1,0:T(8,128)(2,1)S(1)} %copy-done.6, f32[1024]{0:T(1024)S(1)} %bitcast.95, f32[1024]{0:T(1024)S(1)} %add_rsqrt_fusion.1, f32[2048]{0:T(1024)S(1)} %bitcast.91), kind=kOutput, calls=%fused_computation.17 | convolution fusion | flops 8600420352 | bytes 20987904 | tf_op jit(solution)/shard_map/dot_general | solution.py:46
  226.2 0.0 reduce-scatter.5.cloned.1.call-update
  226.2 0.7 copy-done.9
  226.9 0.1 eq.86
  227.0 0.1 eq.82
  227.1 0.8 copy-done.4
  227.9 0.5 fusion.20
  228.4 0.1 rsqrt.44
  228.5 0.0 copy-done.11
  228.5 0.1 eq.95
  228.6 0.1 eq.91
  228.6 0.5 fusion.22
  229.2 1.0 copy-done.5
  230.2 9.6 %bitcast_add_fusion = f32[512,2048]{1,0:T(8,128)} fusion(bf16[1,2,16,16,2048]{4,3,2,1,0:T(8,128)(2,1)S(1)} %copy-done.5, bf16[512,2048]{1,0:T(8,128)(2,1)S(1)} %fusion.22, bf16[1,2048,2048]{2,1,0:T(8,128)(2,1)} %all-gather.10.cloned.1.call-done), kind=kOutput, calls=%fused_computation.18 | convolution fusion | flops 4297064448 | bytes 16777216 | tf_op jit(solution)/shard_map/dot_general | solution.py:36
  239.9 43.5 %reduce-scatter.3.cloned.1.call-done = f32[256,2048]{1,0:T(8,128)} async-done(((f32[1024,2048]{1,0:T(8,128)}), f32[256,2048]{1,0:T(8,128)}) %reduce-scatter.3.cloned.1.call-update) | async-done | bytes 2097168 | tf_op jit(solution)/shard_map/reduce_scatter | solution.py:51
  283.4 0.0 copy-done
  283.4 4.2 multiply_reduce_fusion.1
  287.6 70.1 %reduce-scatter.5.cloned.1.call-done = f32[256,2048]{1,0:T(8,128)} async-done(((f32[1024,2048]{1,0:T(8,128)}), f32[256,2048]{1,0:T(8,128)}) %reduce-scatter.5.cloned.1.call-update) | async-done | bytes 2097168 | tf_op jit(solution)/shard_map/reduce_scatter | solution.py:51
  357.7 3.1 multiply_reduce_fusion
  360.8 0.4 multiply_convert_fusion.1
  361.3 8.8 %copy.27 = bf16[16,16,2048]{0,1,2:T(8,128)(2,1)} copy(bf16[16,16,2048]{2,1,0:T(8,128)(2,1)S(1)} %bitcast.87) | data formatting | bytes 2097152 | tf_op jit(solution)/shard_map/reshape | solution.py:68
  370.1 0.0 copy-done.8
  370.1 7.5 %bitcast_bitcast_fusion = bf16[2048,16,16]{2,1,0:T(8,128)(2,1)} fusion(bf16[16,16,2048]{0,1,2:T(8,128)(2,1)} %copy.27), kind=kLoop, calls=%fused_computation.71 | loop fusion | bytes 2097152
  377.6 11.2 %reshape.107 = bf16[8,2,32768]{2,1,0:T(2,128)(2,1)} reshape(bf16[2048,16,16]{2,1,0:T(8,128)(2,1)} %bitcast_bitcast_fusion) | data formatting | bytes 2097152
  388.8 5.5 %all-to-all-start.1 = ((bf16[8,2,32768]{2,1,0:T(2,128)(2,1)}), bf16[8,2,32768]{2,1,0:T(2,128)(2,1)S(1)}, u32[]{:S(2)}, u32[]{:S(2)}) async-start(bf16[8,2,32768]{2,1,0:T(2,128)(2,1)} %reshape.107), calls=%async_computation.3 | async-start | bytes 2097152 | tf_op jit(solution)/shard_map/all_to_all | solution.py:69
  394.3 8.8 %copy.24 = bf16[16,16,2048]{0,1,2:T(8,128)(2,1)} copy(bf16[16,16,2048]{2,1,0:T(8,128)(2,1)S(1)} %bitcast.86) | data formatting | bytes 2097152 | tf_op jit(solution)/shard_map/reshape | solution.py:68
  403.1 7.5 %bitcast_bitcast_fusion.1 = bf16[2048,16,16]{2,1,0:T(8,128)(2,1)} fusion(bf16[16,16,2048]{0,1,2:T(8,128)(2,1)} %copy.24), kind=kLoop, calls=%fused_computation.72 | loop fusion | bytes 2097152
  410.6 11.2 %reshape.109 = bf16[8,2,32768]{2,1,0:T(2,128)(2,1)} reshape(bf16[2048,16,16]{2,1,0:T(8,128)(2,1)} %bitcast_bitcast_fusion.1) | data formatting | bytes 2097152
  421.8 0.0 all-to-all-done.1
  421.8 6.0 %all-to-all-start = ((bf16[8,2,32768]{2,1,0:T(2,128)(2,1)}), bf16[8,2,32768]{2,1,0:T(2,128)(2,1)S(1)}, u32[]{:S(2)}, u32[]{:S(2)}) async-start(bf16[8,2,32768]{2,1,0:T(2,128)(2,1)} %reshape.109), calls=%async_computation.1 | async-start | bytes 2097152 | tf_op jit(solution)/shard_map/all_to_all | solution.py:69
  427.9 3.9 fusion.30
  431.8 0.1 stack_reshape.7
  431.9 4.0 fusion.29
  435.9 0.1 stack_reshape.6
  435.9 0.7 maximum_bitcast_fusion.1
  436.6 7.5 %reshape.108 = bf16[2048,16,16]{2,1,0:T(8,128)(2,1)} reshape(bf16[8,2,32768]{2,1,0:T(2,128)(2,1)S(1)} %all-to-all-done.1) | data formatting | bytes 2097152
  444.1 9.1 %copy.29 = bf16[16,256,8,16]{1,3,2,0:T(8,128)(2,1)} copy(bf16[16,256,8,16]{3,0,1,2:T(8,128)(2,1)} %bitcast.80) | data formatting | bytes 2097152 | tf_op jit(solution)/shard_map/all_to_all | solution.py:69
  453.2 0.0 all-to-all-done
  453.3 7.5 %reshape.110 = bf16[2048,16,16]{2,1,0:T(8,128)(2,1)} reshape(bf16[8,2,32768]{2,1,0:T(2,128)(2,1)S(1)} %all-to-all-done) | data formatting | bytes 2097152
  460.8 9.1 %copy.26 = bf16[16,256,8,16]{1,3,2,0:T(8,128)(2,1)} copy(bf16[16,256,8,16]{3,0,1,2:T(8,128)(2,1)} %bitcast.81) | data formatting | bytes 2097152 | tf_op jit(solution)/shard_map/all_to_all | solution.py:69
  469.9 1.7 maximum_bitcast_fusion
  471.7 2.4 copy.30
  (31 shorter events, 0.1 us)
Async XLA Ops:
  7.2 276.2 %copy-start = (bf16[256,2048]{1,0:T(8,128)(2,1)S(1)}, bf16[256,2048]{1,0:T(8,128)(2,1)}, u32[]{:S(2)}) copy-start(bf16[256,2048]{1,0:T(8,128)(2,1)} %param.16) | copy-start | bytes 3145732
  7.2 4.8 %copy-start.13 = (s32[1,2]{1,0:T(1,128)S(1)}, s32[1,2]{1,0:T(1,128)}, u32[]{:S(2)}) copy-start(s32[1,2]{1,0:T(1,128)} %param.13) | copy-start | bytes 28
  7.2 11.0 %copy-start.10 = (bf16[1,2048]{1,0:T(2,128)(2,1)S(1)}, bf16[1,2048]{1,0:T(2,128)(2,1)}, u32[]{:S(2)}) copy-start(bf16[1,2048]{1,0:T(2,128)(2,1)} %param.15) | copy-start | bytes 12292
  7.2 40.6 %all-gather.6.cloned.1.call-start = ((), (), s32[]{:S(2)}) async-start(), calls=%async_computation.4 | async-start | bytes 5242880 | tf_op jit(solution)/shard_map/all_gather | solution.py:44
  10.5 164.4 %all-gather.10.cloned.1.call-start = ((), (), s32[]{:S(2)}) async-start(), calls=%async_computation.8 | async-start | bytes 9437184 | tf_op jit(solution)/shard_map/all_gather | solution.py:35
  11.2 197.9 %all-gather.8.cloned.1.call-start = ((), (), s32[]{:S(2)}) async-start(), calls=%async_computation.6 | async-start | bytes 5242880 | tf_op jit(solution)/shard_map/all_gather | solution.py:44
  12.0 271.4 %reduce-scatter.3.cloned.1.call-start = ((), (), s32[]{:S(2)}) async-start(), calls=%async_computation.5 | async-start | bytes 10485760 | tf_op jit(solution)/shard_map/reduce_scatter | solution.py:51
  189.5 168.2 %reduce-scatter.5.cloned.1.call-start = ((), (), s32[]{:S(2)}) async-start(), calls=%async_computation.7 | async-start | bytes 10485760 | tf_op jit(solution)/shard_map/reduce_scatter | solution.py:51
  209.2 3.4 copy-start.6
  226.2 0.8 copy-start.9
  226.2 1.7 copy-start.4
  226.2 2.3 copy-start.11
  228.6 1.6 copy-start.5
  230.2 53.1 %copy-start.2 = (bf16[1,1,16,16,2048]{4,3,2,1,0:T(8,128)(2,1)S(1)}, bf16[1,1,16,16,2048]{4,3,2,1,0:T(8,128)(2,1)}, u32[]{:S(2)}) copy-start(bf16[1,1,16,16,2048]{4,3,2,1,0:T(8,128)(2,1)} %get-tuple-element.8) | copy-start | bytes 3145732
  239.9 117.8 %copy-start.1 = (bf16[1,1,16,16,2048]{4,3,2,1,0:T(8,128)(2,1)S(1)}, bf16[1,1,16,16,2048]{4,3,2,1,0:T(8,128)(2,1)}, u32[]{:S(2)}) copy-start(bf16[1,1,16,16,2048]{4,3,2,1,0:T(8,128)(2,1)} %get-tuple-element.9) | copy-start | bytes 3145732
  357.7 3.1 copy-start.3
  361.2 8.8 %copy-start.8 = (bf16[256,2048]{1,0:T(8,128)(2,1)}, bf16[256,2048]{1,0:T(8,128)(2,1)S(1)}, u32[]{:S(2)}) copy-start(bf16[256,2048]{1,0:T(8,128)(2,1)S(1)} %get-tuple-element.15) | copy-start | bytes 3145732
  361.3 33.1 %copy-start.7 = (bf16[256,2048]{1,0:T(8,128)(2,1)}, bf16[256,2048]{1,0:T(8,128)(2,1)S(1)}, u32[]{:S(2)}) copy-start(bf16[256,2048]{1,0:T(8,128)(2,1)S(1)} %get-tuple-element.14) | copy-start | bytes 3145732
  388.8 33.0 %all-to-all-start.1 = ((bf16[8,2,32768]{2,1,0:T(2,128)(2,1)}), bf16[8,2,32768]{2,1,0:T(2,128)(2,1)S(1)}, u32[]{:S(2)}, u32[]{:S(2)}) async-start(bf16[8,2,32768]{2,1,0:T(2,128)(2,1)} %reshape.107), calls=%async_computation.3 | async-start | bytes 2097152 | tf_op jit(solution)/shard_map/all_to_all | solution.py:69
  410.6 17.2 %copy-start.12 = (bf16[1024]{0:T(1024)(128)(2,1)S(1)}, bf16[1024]{0:T(1024)(128)(2,1)}, u32[]{:S(2)}) copy-start(bf16[1024]{0:T(1024)(128)(2,1)} %param.19) | copy-start | bytes 6148
  421.8 31.4 %all-to-all-start = ((bf16[8,2,32768]{2,1,0:T(2,128)(2,1)}), bf16[8,2,32768]{2,1,0:T(2,128)(2,1)S(1)}, u32[]{:S(2)}, u32[]{:S(2)}) async-start(bf16[8,2,32768]{2,1,0:T(2,128)(2,1)} %reshape.109), calls=%async_computation.1 | async-start | bytes 2097152 | tf_op jit(solution)/shard_map/all_to_all | solution.py:69
Sparse Core Ops, SparseCore 0:
  10.6 37.1 all-gather.5
  49.9 124.9 all-gather.9
  176.5 32.6 all-gather.7
  211.6 71.7 reduce-scatter.2
  286.0 71.6 reduce-scatter.4
where the time goes:
time: 482 us; the launch traced here: 481 us
  waiting for transfers between devices  288 us (60%)
  local copies, waits for them, and re-layouts  97.5 us (20%)
  matrix products  52.9 us (11%)
  between operations  13.9 us (3%)
  starting transfers between devices  11.9 us (2%)
  other arithmetic  10.2 us (2%)
  blocking collectives  5.95 us (1%)
    all_gather x1, waiting for transfers between devices, local(): own_whole = lax.all_gather(weight_shard, 'env', axis=0, tiled=True)  124 us
    reduce_scatter x2, waiting for transfers between devices, local(): lax.psum_scatter(products, 'league', scatter_dimension=0, tiled=True)  114 us
    unnamed x39, local copies, waits for them, and re-layouts  57.8 us
    all_gather x2, waiting for transfers between devices, local(): all_rows = lax.all_gather(opp_raw, 'league', axis=0, tiled=True)  49.1 us
    dot_general x2, matrix products, local(): jnp.dot(all_normed, own_whole, preferred_element_type=jnp.float32)  28.1 us
    all_to_all x2, local copies, waits for them, and re-layouts, local(): lax.all_to_all(time_block, 'env', split_axis=1, concat_axis=2, tiled=True)  18.2 us
    reshape x2, local copies, waits for them, and re-layouts, local(): joint_row.reshape(env_count, step_count, model_width).transpose(1, 2, 0)  17.6 us
    all_to_all x2, starting transfers between devices, local(): lax.all_to_all(time_block, 'env', split_axis=1, concat_axis=2, tiled=True)  11.5 us
  transfers between devices with their start and end apart: 7, of which 5 were waited for; matrix products, arithmetic and copies ran while one was open for 21% of the time, Pallas kernels for 0%

commit v1 on v0

--- a/solution.py
+++ b/solution.py
@@ -41,7 +41,16 @@
     for round_index in range(round_count):
         opp_raw = obs_opp[0, round_index].reshape(row_count, model_width)
         opp_inputs = opp_raw.astype(jnp.float32)
-        all_rows = lax.all_gather(opp_raw, "league", axis=0, tiled=True)
+        ring = [opp_raw]
+        for hop in range(3):
+            ring.append(
+                lax.ppermute(ring[-1], "league", [(dev, (dev + 1) % 4) for dev in range(4)])
+            )
+        all_rows = jnp.roll(
+            jnp.concatenate(ring[::-1], axis=0),
+            (lax.axis_index("league") + 1) * ring[0].shape[0],
+            axis=0,
+        )
         all_normed = rms_norm(all_rows.astype(jnp.float32), own_gain).astype(jnp.bfloat16)
         products = jnp.dot(all_normed, own_whole, preferred_element_type=jnp.float32)
         served = (every_pick[:, round_index] == my_group).astype(jnp.float32)

time: 482 us -> 421 us (0.87)
  waiting for transfers between devices: 288 us -> 195 us
  blocking collectives: 5.95 us -> 23.2 us
  other arithmetic: 10.2 us -> 24.5 us
    all_gather x1, waiting for transfers between devices: 124 us -> 38.8 us  [local(): own_whole = lax.all_gather(weight_shard, 'env', axis=0, tiled=True)]
    all_gather x2 -> x0, waiting for transfers between devices: 49.1 us -> none  [local(): all_rows = lax.all_gather(opp_raw, 'league', axis=0, tiled=True)]
    ppermute x0 -> x6, waiting for transfers between devices: none -> 45.6 us  [local(): lax.ppermute(ring[-1], 'league', [(dev, (dev + 1) % 4) for dev in range(4)])]
    all_gather x1, blocking collectives: 5.95 us -> 23.2 us  [local(): every_pick = lax.all_gather(opponent_picks, 'league', axis=0, tiled=True)]
    reduce_sum x3 -> x2, other arithmetic: 6.75 us -> 19.3 us  [rms_norm(): scale = lax.rsqrt(jnp.mean(inputs * inputs, axis=-1, keepdims=True) + 1e-05)]
    unnamed x39 -> x35, local copies, waits for them, and re-layouts: 57.8 us -> 55.8 us
  transfers between devices with their start and end apart: 7 -> 11, of which waited for: 5 -> 7; matrix products, arithmetic and copies ran while one was open for 21% -> 25% of each run, Pallas kernels for 0% -> 0%
where the time goes in v1:
time: 421 us; the launch traced here: 420 us
  waiting for transfers between devices  195 us (46%)
  local copies, waits for them, and re-layouts  94 us (22%)
  matrix products  54.8 us (13%)
  other arithmetic  24.5 us (6%)
  blocking collectives  23.2 us (6%)
  starting transfers between devices  14.9 us (4%)
  between operations  13.9 us (3%)
    reduce_scatter x2, waiting for transfers between devices, local(): lax.psum_scatter(products, 'league', scatter_dimension=0, tiled=True)  110 us
    unnamed x35, local copies, waits for them, and re-layouts  55.8 us
    ppermute x6, waiting for transfers between devices, local(): lax.ppermute(ring[-1], 'league', [(dev, (dev + 1) % 4) for dev in range(4)])  45.6 us
    all_gather x1, waiting for transfers between devices, local(): own_whole = lax.all_gather(weight_shard, 'env', axis=0, tiled=True)  38.8 us
    dot_general x2, matrix products, local(): jnp.dot(all_normed, own_whole, preferred_element_type=jnp.float32)  29.4 us
    all_gather x1, blocking collectives, local(): every_pick = lax.all_gather(opponent_picks, 'league', axis=0, tiled=True)  23.2 us
    reduce_sum x2, other arithmetic, rms_norm(): scale = lax.rsqrt(jnp.mean(inputs * inputs, axis=-1, keepdims=True) + 1e-05)  19.3 us
    all_to_all x2, local copies, waits for them, and re-layouts, local(): lax.all_to_all(time_block, 'env', split_axis=1, concat_axis=2, tiled=True)  18.2 us
  transfers between devices with their start and end apart: 11, of which 7 were waited for; matrix products, arithmetic and copies ran while one was open for 25% of the time, Pallas kernels for 0%

profile of v1, /device:TPU:0, one launch (start us, length us, event | category | flops | bytes accessed | tf_op | source)
XLA Modules:
  0.0 420.0 jit_solution(4237781082797897207)
XLA Ops:
  7.2 0.0 copy-start
  7.2 0.0 all-gather.4.cloned.1.call-start
  7.2 0.7 all-gather.4.cloned.1.call-update
  7.9 0.0 reduce-scatter.3.cloned.1.call-start
  8.0 1.7 fusion.65
  9.7 0.5 collective-permute-start
  10.2 2.6 collective-permute-start.3
  12.8 11.8 %collective-permute-done = bf16[256,2048]{1,0:T(8,128)(2,1)S(1)} collective-permute-done((bf16[256,2048]{1,0:T(8,128)(2,1)S(1)}, bf16[256,2048]{1,0:T(8,128)(2,1)S(1)}, u32[]{:S(2)}, u32[]{:S(2)}) %collective-permute-start) | collective-permute-done | bytes 1048608 | tf_op jit(solution)/shard_map/ppermute | solution.py:47
  24.6 0.0 collective-permute-start.1
  24.6 11.2 %collective-permute-done.3 = bf16[256,2048]{1,0:T(8,128)(2,1)S(1)} collective-permute-done((bf16[256,2048]{1,0:T(8,128)(2,1)S(1)}, bf16[256,2048]{1,0:T(8,128)(2,1)S(1)}, u32[]{:S(2)}, u32[]{:S(2)}) %collective-permute-start.3) | collective-permute-done | bytes 1048608 | tf_op jit(solution)/shard_map/ppermute | solution.py:47
  35.8 0.0 collective-permute-start.4
  35.8 11.3 %collective-permute-done.1 = bf16[256,2048]{1,0:T(8,128)(2,1)} collective-permute-done((bf16[256,2048]{1,0:T(8,128)(2,1)S(1)}, bf16[256,2048]{1,0:T(8,128)(2,1)}, u32[]{:S(2)}, u32[]{:S(2)}) %collective-permute-start.1) | collective-permute-done | bytes 1048608 | tf_op jit(solution)/shard_map/ppermute | solution.py:47
  47.2 0.0 copy-done.6
  47.2 0.0 collective-permute-start.2
  47.2 11.2 %collective-permute-done.4 = bf16[256,2048]{1,0:T(8,128)(2,1)} collective-permute-done((bf16[256,2048]{1,0:T(8,128)(2,1)S(1)}, bf16[256,2048]{1,0:T(8,128)(2,1)}, u32[]{:S(2)}, u32[]{:S(2)}) %collective-permute-start.4) | collective-permute-done | bytes 1048608 | tf_op jit(solution)/shard_map/ppermute | solution.py:47
  58.4 0.0 collective-permute-start.5
  58.4 0.0 copy-done.11
  58.4 23.2 %all-gather.1 = s32[4,1,2]{2,1,0:T(1,128)S(1)} all-gather(s32[1,1,2]{2,1,0:T(1,128)S(1)} %bitcast.100), channel_id=1, replica_groups=mesh['league'=4,'env'=8] {'league'}, dimensions={0}, use_global_device_ids=true | all-gather | bytes 40 | tf_op jit(solution)/shard_map/all_gather | solution.py:37
  81.6 0.1 copy.23
  81.7 0.1 broadcast_bitcast_fusion
  81.8 0.0 collective-permute-done.2
  81.8 0.0 collective-permute-done.5
  81.8 17.3 %fusion = (f32[1024]{0:T(1024)S(1)}, bf16[1024,2048]{1,0:T(8,128)(2,1)}, f32[1024]{0:T(1024)S(1)}, bf16[1024,2048]{1,0:T(8,128)(2,1)}) fusion(s32[]{:T(128)S(6)} %select_n.13, bf16[256,2048]{1,0:T(8,128)(2,1)S(1)} %bitcast.86, bf16[256,2048]{1,0:T(8,128)(2,1)} %copy-done.5, bf16[256,2048]{1,0:T(8,128)(2,1)} %collective-permute-done.1, ...), kind=kLoop, calls=%fused_computation.4 | loop fusion | flops 79689728 | bytes 16785412 | tf_op jit(solution)/shard_map/reduce_sum | solution.py:8
  99.1 38.8 %all-gather.4.cloned.1.call-done = bf16[1,2048,2048]{2,1,0:T(8,128)(2,1)} async-done(((bf16[1,256,2048]{2,1,0:T(8,128)(2,1)}), bf16[1,2048,2048]{2,1,0:T(8,128)(2,1)}) %all-gather.4.cloned.1.call-update) | async-done | bytes 8388624 | tf_op jit(solution)/shard_map/all_gather | solution.py:35
  137.8 14.6 %fusion.12 = f32[1024,2048]{1,0:T(8,128)} fusion(bf16[1,2048,2048]{2,1,0:T(8,128)(2,1)} %all-gather.4.cloned.1.call-done, bf16[1024,2048]{1,0:T(8,128)(2,1)} %get-tuple-element.10, f32[1024]{0:T(1024)S(1)} %bitcast.96, f32[2048]{0:T(1024)S(1)} %bitcast.92, f32[1024]{0:T(1024)S(1)} %add_rsqrt_fusion.2), kind=kOutput, calls=%fused_computation.32 | convolution fusion | flops 8600420352 | bytes 20987904 | tf_op jit(solution)/shard_map/dot_general | solution.py:55
  152.5 0.0 reduce-scatter.3.cloned.1.call-update
  152.5 0.2 reduce-scatter.5.cloned.1.call-start
  152.7 14.7 %fusion.15 = f32[1024,2048]{1,0:T(8,128)} fusion(bf16[1,2048,2048]{2,1,0:T(8,128)(2,1)} %all-gather.4.cloned.1.call-done, bf16[1024,2048]{1,0:T(8,128)(2,1)} %get-tuple-element.28, f32[1024]{0:T(1024)S(1)} %bitcast.97, f32[1024]{0:T(1024)S(1)} %add_rsqrt_fusion.1, f32[2048]{0:T(1024)S(1)} %bitcast.93), kind=kOutput, calls=%fused_computation.33 | convolution fusion | flops 8600420352 | bytes 20987904 | tf_op jit(solution)/shard_map/dot_general | solution.py:55
  167.5 0.0 reduce-scatter.5.cloned.1.call-update
  167.5 0.7 copy-done.7
  168.2 0.1 eq.88
  168.3 0.1 eq.84
  168.4 2.1 fusion.34
  170.5 0.1 rsqrt.44
  170.6 0.1 eq.97
  170.7 0.1 eq.93
  170.8 2.3 fusion.36
  173.1 10.2 %bitcast_add_fusion = f32[512,2048]{1,0:T(8,128)} fusion(bf16[1,2,16,16,2048]{4,3,2,1,0:T(8,128)(2,1)S(1)} %copy-done.2, bf16[512,2048]{1,0:T(8,128)(2,1)S(1)} %fusion.36, bf16[1,2048,2048]{2,1,0:T(8,128)(2,1)} %all-gather.4.cloned.1.call-done), kind=kOutput, calls=%fused_computation.48 | convolution fusion | flops 4297064448 | bytes 16777216 | tf_op jit(solution)/shard_map/dot_general | solution.py:36
  183.3 39.3 %reduce-scatter.3.cloned.1.call-done = f32[256,2048]{1,0:T(8,128)} async-done(((f32[1024,2048]{1,0:T(8,128)}), f32[256,2048]{1,0:T(8,128)}) %reduce-scatter.3.cloned.1.call-update) | async-done | bytes 2097168 | tf_op jit(solution)/shard_map/reduce_scatter | solution.py:60
  222.6 4.2 multiply_reduce_fusion.1
  226.7 70.3 %reduce-scatter.5.cloned.1.call-done = f32[256,2048]{1,0:T(8,128)} async-done(((f32[1024,2048]{1,0:T(8,128)}), f32[256,2048]{1,0:T(8,128)}) %reduce-scatter.5.cloned.1.call-update) | async-done | bytes 2097168 | tf_op jit(solution)/shard_map/reduce_scatter | solution.py:60
  297.1 3.1 multiply_reduce_fusion
  300.2 0.4 multiply_convert_fusion.1
  300.6 8.8 %copy.27 = bf16[16,16,2048]{0,1,2:T(8,128)(2,1)} copy(bf16[16,16,2048]{2,1,0:T(8,128)(2,1)S(1)} %bitcast.89) | data formatting | bytes 2097152 | tf_op jit(solution)/shard_map/reshape | solution.py:77
  309.5 7.5 %bitcast_bitcast_fusion = bf16[2048,16,16]{2,1,0:T(8,128)(2,1)} fusion(bf16[16,16,2048]{0,1,2:T(8,128)(2,1)} %copy.27), kind=kLoop, calls=%fused_computation.101 | loop fusion | bytes 2097152
  316.9 11.2 %reshape.107 = bf16[8,2,32768]{2,1,0:T(2,128)(2,1)} reshape(bf16[2048,16,16]{2,1,0:T(8,128)(2,1)} %bitcast_bitcast_fusion) | data formatting | bytes 2097152
  328.2 5.5 %all-to-all-start.1 = ((bf16[8,2,32768]{2,1,0:T(2,128)(2,1)}), bf16[8,2,32768]{2,1,0:T(2,128)(2,1)S(1)}, u32[]{:S(2)}, u32[]{:S(2)}) async-start(bf16[8,2,32768]{2,1,0:T(2,128)(2,1)} %reshape.107), calls=%async_computation.3 | async-start | bytes 2097152 | tf_op jit(solution)/shard_map/all_to_all | solution.py:78
  333.7 8.8 %copy.24 = bf16[16,16,2048]{0,1,2:T(8,128)(2,1)} copy(bf16[16,16,2048]{2,1,0:T(8,128)(2,1)S(1)} %bitcast.88) | data formatting | bytes 2097152 | tf_op jit(solution)/shard_map/reshape | solution.py:77
  342.5 7.5 %bitcast_bitcast_fusion.1 = bf16[2048,16,16]{2,1,0:T(8,128)(2,1)} fusion(bf16[16,16,2048]{0,1,2:T(8,128)(2,1)} %copy.24), kind=kLoop, calls=%fused_computation.102 | loop fusion | bytes 2097152
  350.0 11.2 %reshape.109 = bf16[8,2,32768]{2,1,0:T(2,128)(2,1)} reshape(bf16[2048,16,16]{2,1,0:T(8,128)(2,1)} %bitcast_bitcast_fusion.1) | data formatting | bytes 2097152
  361.2 0.0 all-to-all-done.1
  361.2 6.0 %all-to-all-start = ((bf16[8,2,32768]{2,1,0:T(2,128)(2,1)}), bf16[8,2,32768]{2,1,0:T(2,128)(2,1)S(1)}, u32[]{:S(2)}, u32[]{:S(2)}) async-start(bf16[8,2,32768]{2,1,0:T(2,128)(2,1)} %reshape.109), calls=%async_computation.1 | async-start | bytes 2097152 | tf_op jit(solution)/shard_map/all_to_all | solution.py:78
  367.2 3.9 fusion.44
  371.2 0.1 stack_reshape.7
  371.3 4.0 fusion.43
  375.2 0.1 stack_reshape.6
  375.3 0.7 maximum_bitcast_fusion.1
  376.0 7.6 %reshape.108 = bf16[2048,16,16]{2,1,0:T(8,128)(2,1)} reshape(bf16[8,2,32768]{2,1,0:T(2,128)(2,1)S(1)} %all-to-all-done.1) | data formatting | bytes 2097152
  383.5 9.1 %copy.29 = bf16[16,256,8,16]{1,3,2,0:T(8,128)(2,1)} copy(bf16[16,256,8,16]{3,0,1,2:T(8,128)(2,1)} %bitcast.80) | data formatting | bytes 2097152 | tf_op jit(solution)/shard_map/all_to_all | solution.py:78
  392.6 0.0 all-to-all-done
  392.7 7.6 %reshape.110 = bf16[2048,16,16]{2,1,0:T(8,128)(2,1)} reshape(bf16[8,2,32768]{2,1,0:T(2,128)(2,1)S(1)} %all-to-all-done) | data formatting | bytes 2097152
  400.2 9.1 %copy.26 = bf16[16,256,8,16]{1,3,2,0:T(8,128)(2,1)} copy(bf16[16,256,8,16]{3,0,1,2:T(8,128)(2,1)} %bitcast.81) | data formatting | bytes 2097152 | tf_op jit(solution)/shard_map/all_to_all | solution.py:78
  409.3 1.7 maximum_bitcast_fusion
  411.1 2.4 copy.30
  (32 shorter events, 0.1 us)
Async XLA Ops:
  7.2 215.4 %copy-start = (bf16[256,2048]{1,0:T(8,128)(2,1)S(1)}, bf16[256,2048]{1,0:T(8,128)(2,1)}, u32[]{:S(2)}) copy-start(bf16[256,2048]{1,0:T(8,128)(2,1)} %param.18) | copy-start | bytes 3145732
  7.2 51.2 %copy-start.11 = (s32[1,2]{1,0:T(1,128)S(1)}, s32[1,2]{1,0:T(1,128)}, u32[]{:S(2)}) copy-start(s32[1,2]{1,0:T(1,128)} %param.15) | copy-start | bytes 28
  7.2 74.6 %copy-start.8 = (bf16[1,2048]{1,0:T(2,128)(2,1)S(1)}, bf16[1,2048]{1,0:T(2,128)(2,1)}, u32[]{:S(2)}) copy-start(bf16[1,2048]{1,0:T(2,128)(2,1)} %param.17) | copy-start | bytes 12292
  7.2 130.6 %all-gather.4.cloned.1.call-start = ((), (), s32[]{:S(2)}) async-start(), calls=%async_computation.6 | async-start | bytes 9437184 | tf_op jit(solution)/shard_map/all_gather | solution.py:35
  7.9 214.6 %reduce-scatter.3.cloned.1.call-start = ((), (), s32[]{:S(2)}) async-start(), calls=%async_computation.4 | async-start | bytes 10485760 | tf_op jit(solution)/shard_map/reduce_scatter | solution.py:60
  9.7 14.9 %collective-permute-start = (bf16[256,2048]{1,0:T(8,128)(2,1)S(1)}, bf16[256,2048]{1,0:T(8,128)(2,1)S(1)}, u32[]{:S(2)}, u32[]{:S(2)}) collective-permute-start(bf16[256,2048]{1,0:T(8,128)(2,1)S(1)} %bitcast.85), channel_id=1, source_target_pairs={{0,8},{8,16},{16,24},{24,0},{1,9},{9,17},{17,25},{25,1},{2,10},{10... | collective-permute-start | bytes 3145736 | tf_op jit(solution)/shard_map/ppermute | solution.py:47
  10.2 25.6 %collective-permute-start.3 = (bf16[256,2048]{1,0:T(8,128)(2,1)S(1)}, bf16[256,2048]{1,0:T(8,128)(2,1)S(1)}, u32[]{:S(2)}, u32[]{:S(2)}) collective-permute-start(bf16[256,2048]{1,0:T(8,128)(2,1)S(1)} %bitcast.82), channel_id=1, source_target_pairs={{0,8},{8,16},{16,24},{24,0},{1,9},{9,17},{17,25},{25,1},{2,10},{10... | collective-permute-start | bytes 3145736 | tf_op jit(solution)/shard_map/ppermute | solution.py:47
  24.6 11.2 %copy-start.5 = (bf16[256,2048]{1,0:T(8,128)(2,1)}, bf16[256,2048]{1,0:T(8,128)(2,1)S(1)}, u32[]{:S(2)}) copy-start(bf16[256,2048]{1,0:T(8,128)(2,1)S(1)} %collective-permute-done) | copy-start | bytes 3145732
  24.6 22.6 %collective-permute-start.1 = (bf16[256,2048]{1,0:T(8,128)(2,1)S(1)}, bf16[256,2048]{1,0:T(8,128)(2,1)}, u32[]{:S(2)}, u32[]{:S(2)}) collective-permute-start(bf16[256,2048]{1,0:T(8,128)(2,1)S(1)} %collective-permute-done), channel_id=1, source_target_pairs={{0,8},{8,16},{16,24},{24,0},{1,9},{9,17},{17,25},{25,1},{2,10},{10... | collective-permute-start | bytes 3145736 | tf_op jit(solution)/shard_map/ppermute | solution.py:47
  35.8 11.3 %copy-start.6 = (bf16[256,2048]{1,0:T(8,128)(2,1)}, bf16[256,2048]{1,0:T(8,128)(2,1)S(1)}, u32[]{:S(2)}) copy-start(bf16[256,2048]{1,0:T(8,128)(2,1)S(1)} %collective-permute-done.3) | copy-start | bytes 3145732
  35.8 22.6 %collective-permute-start.4 = (bf16[256,2048]{1,0:T(8,128)(2,1)S(1)}, bf16[256,2048]{1,0:T(8,128)(2,1)}, u32[]{:S(2)}, u32[]{:S(2)}) collective-permute-start(bf16[256,2048]{1,0:T(8,128)(2,1)S(1)} %collective-permute-done.3), channel_id=1, source_target_pairs={{0,8},{8,16},{16,24},{24,0},{1,9},{9,17},{17,25},{25,1},{2,10},{10... | collective-permute-start | bytes 3145736 | tf_op jit(solution)/shard_map/ppermute | solution.py:47
  47.2 34.6 %collective-permute-start.2 = (bf16[256,2048]{1,0:T(8,128)(2,1)}, bf16[256,2048]{1,0:T(8,128)(2,1)}, u32[]{:S(2)}, u32[]{:S(2)}) collective-permute-start(bf16[256,2048]{1,0:T(8,128)(2,1)} %collective-permute-done.1), channel_id=1, source_target_pairs={{0,8},{8,16},{16,24},{24,0},{1,9},{9,17},{17,25},{25,1},{2,10},{10... | collective-permute-start | bytes 3145736 | tf_op jit(solution)/shard_map/ppermute | solution.py:47
  58.4 23.4 %collective-permute-start.5 = (bf16[256,2048]{1,0:T(8,128)(2,1)}, bf16[256,2048]{1,0:T(8,128)(2,1)}, u32[]{:S(2)}, u32[]{:S(2)}) collective-permute-start(bf16[256,2048]{1,0:T(8,128)(2,1)} %collective-permute-done.4), channel_id=1, source_target_pairs={{0,8},{8,16},{16,24},{24,0},{1,9},{9,17},{17,25},{25,1},{2,10},{10... | collective-permute-start | bytes 3145736 | tf_op jit(solution)/shard_map/ppermute | solution.py:47
  152.5 144.6 %reduce-scatter.5.cloned.1.call-start = ((), (), s32[]{:S(2)}) async-start(), calls=%async_computation.5 | async-start | bytes 10485760 | tf_op jit(solution)/shard_map/reduce_scatter | solution.py:60
  167.5 0.8 copy-start.7
  167.5 3.1 copy-start.9
  170.7 2.3 copy-start.2
  297.1 3.1 copy-start.1
  300.6 8.8 %copy-start.4 = (bf16[256,2048]{1,0:T(8,128)(2,1)}, bf16[256,2048]{1,0:T(8,128)(2,1)S(1)}, u32[]{:S(2)}) copy-start(bf16[256,2048]{1,0:T(8,128)(2,1)S(1)} %get-tuple-element.20) | copy-start | bytes 3145732
  300.6 33.1 %copy-start.3 = (bf16[256,2048]{1,0:T(8,128)(2,1)}, bf16[256,2048]{1,0:T(8,128)(2,1)S(1)}, u32[]{:S(2)}) copy-start(bf16[256,2048]{1,0:T(8,128)(2,1)S(1)} %get-tuple-element.19) | copy-start | bytes 3145732
  328.2 33.1 %all-to-all-start.1 = ((bf16[8,2,32768]{2,1,0:T(2,128)(2,1)}), bf16[8,2,32768]{2,1,0:T(2,128)(2,1)S(1)}, u32[]{:S(2)}, u32[]{:S(2)}) async-start(bf16[8,2,32768]{2,1,0:T(2,128)(2,1)} %reshape.107), calls=%async_computation.3 | async-start | bytes 2097152 | tf_op jit(solution)/shard_map/all_to_all | solution.py:78
  350.0 17.2 %copy-start.10 = (bf16[1024]{0:T(1024)(128)(2,1)S(1)}, bf16[1024]{0:T(1024)(128)(2,1)}, u32[]{:S(2)}) copy-start(bf16[1024]{0:T(1024)(128)(2,1)} %param.21) | copy-start | bytes 6148
  361.2 31.4 %all-to-all-start = ((bf16[8,2,32768]{2,1,0:T(2,128)(2,1)}), bf16[8,2,32768]{2,1,0:T(2,128)(2,1)S(1)}, u32[]{:S(2)}, u32[]{:S(2)}) async-start(bf16[8,2,32768]{2,1,0:T(2,128)(2,1)} %reshape.109), calls=%async_computation.1 | async-start | bytes 2097152 | tf_op jit(solution)/shard_map/all_to_all | solution.py:78
Sparse Core Ops, SparseCore 0:
  10.2 127.6 all-gather.3
  152.6 69.8 reduce-scatter.2
  225.3 71.6 reduce-scatter.4
